TPU v7x, 256 devices: a whole 4x4x8 slice. The times are simulated.
256 devices in a mesh: set: 32 (over y, x, core), path: 8 (over z).
Axes of the slice: x: 4, y: 4, z: 8, core: 2. Of those that a mesh axis runs over, the one named last changes fastest.
Arguments:
- start_state: float32 [4096, 2048], P(('path', 'set')), may hold values from -6 to 6
- shocks: bfloat16 [2, 4096, 2048], P(None, ('path', 'set')), may hold values from -6 to 6
- loading: bfloat16 [2048, 2048], replicated, may hold values from -0.125 to 0.125
- decay: float32 [2048], replicated, may hold values from 0.5 to 1
- factor_lists: int32 [4096, 64], P('set'), may hold values from 0 to 2047, all different within a row
- delta: bfloat16 [4096, 64], P('set'), may hold values from -0.75 to 0.75
- gamma: bfloat16 [4096, 64, 64], P('set'), may hold values from -0.09375 to 0.09375
- currency: int32 [4096], P('set'), may hold values from 0 to 15
- owner: int32 [4096], P('set'), may hold values from 0 to 255
Outputs:
- exposure: float32 [2, 256, 4096], P(None, 'set', 'path')
- end_state: float32 [4096, 2048], P(('path', 'set'))
Inputs may be any that keep to these rules, and one draw needn't show every extreme that they name: `factor_lists`: the 64 factors of one netting set are different.
All inputs are finite; a program needn't handle non-finite values.
Results may differ from a plain program's by a relative error of at most 0.004.
Values may be sent and summed in bfloat16 or wider, within the bound.
No kernel may reach another device: no remote copies, remote signals or barrier semaphores. Data moves between devices by JAX's collectives and lax.ppermute only.
A program may use at most 64 MiB of HBM per device.

v0:
```python
import math
import jax
import jax.numpy as jnp
from jax import lax
from jax.sharding import PartitionSpec as P

NB = 16
STEPS = 2
PDEV = 16
CP_DEV = 8


def value_block(slab, lists_b, delta_b, gamma_b, cur_b):
    rows = slab.shape[0]
    count = lists_b.shape[0]
    picked = jnp.take(slab, lists_b.reshape(-1), axis=1).reshape(rows, count, lists_b.shape[1])
    curved = jnp.einsum("psk,skl->psl", picked, gamma_b, preferred_element_type=jnp.float32)
    linear = delta_b.astype(jnp.float32)[None] + 0.5 * curved
    local = jnp.sum(picked.astype(jnp.float32) * linear, axis=2)
    rates = jnp.exp(0.2 * jnp.take(slab, cur_b, axis=1).astype(jnp.float32))
    return (local * rates).T


def revalue(slab, lists, delta, gamma, cur):
    total = lists.shape[0]
    width = math.gcd(16, total)
    blocks = total // width
    depth = lists.shape[1]
    stacked = lax.map(
        lambda a: value_block(slab, a[0], a[1], a[2], a[3]),
        (
            lists.reshape(blocks, width, depth),
            delta.reshape(blocks, width, depth),
            gamma.reshape(blocks, width, depth, depth),
            cur.reshape(blocks, width),
        ),
    )
    return stacked.reshape(total, slab.shape[0])


def regress(gram, moments, total):
    size = gram.shape[0]
    chol = jnp.linalg.cholesky(gram / total + 0.001 * jnp.eye(size, dtype=jnp.float32))
    middle = lax.linalg.triangular_solve(chol, moments / total, left_side=True, lower=True)
    return lax.linalg.triangular_solve(chol, middle, left_side=True, lower=True, transpose_a=True)


def per_device(start_state, shocks, loading, decay, factor_lists, delta, gamma, currency, owner):
    high = lax.Precision.HIGHEST
    groups = lax.axis_size("set")
    member = lax.axis_index("set")
    total_paths = PDEV * groups * lax.axis_size("path")
    set_count = factor_lists.shape[0]
    onehot = (owner[None, :] == jnp.arange(CP_DEV * groups, dtype=jnp.int32)[:, None]).astype(
        jnp.float32
    )
    state = start_state
    slabs = []
    evaluated = []
    for step in range(STEPS):
        state = decay[None, :] * state + jnp.dot(
            shocks[step], loading, preferred_element_type=jnp.float32
        )
        slab = state.astype(jnp.bfloat16)
        slabs.append(slab)
        piece = lax.all_gather(slab, "set", axis=0, tiled=True)
        evaluate_values = revalue(piece, factor_lists, delta, gamma, currency)
        evaluated.append(
            jnp.concatenate([evaluate_values, piece[:, :NB].astype(jnp.float32).T], axis=0)
        )
    results = []
    for step in range(STEPS):
        values = evaluated[step][:set_count]
        factors = evaluated[step][set_count:]
        summed = lax.psum(jnp.dot(onehot, values, precision=high), "set")
        netted = lax.dynamic_slice_in_dim(summed, member * CP_DEV, CP_DEV, 0)
        ones = jnp.ones((1, values.shape[1]), jnp.float32)
        basis = jnp.concatenate([ones, factors], axis=0)
        gram, moments = lax.psum(
            (jnp.dot(basis, basis.T, precision=high), jnp.dot(basis, netted.T, precision=high)),
            "path",
        )
        coef = regress(gram, moments, total_paths)
        fitted = jnp.dot(coef.T, basis, precision=high)
        results.append(jnp.maximum(netted - 0.9 * fitted, 0.0))
    return (jnp.stack(results), state)


def solution(mesh):
    return jax.shard_map(
        per_device,
        mesh=mesh,
        in_specs=(
            P(("path", "set"), None),
            P(None, ("path", "set"), None),
            P(),
            P(),
            P("set", None),
            P("set", None),
            P("set", None, None),
            P("set"),
            P("set"),
        ),
        out_specs=(P(None, "set", "path"), P(("path", "set"), None)),
        check_vma=False,
    )
```

profile of v0, /device:TPU:6, one launch (start us, length us, event | category | flops | bytes accessed | tf_op | source)
XLA Modules:
  0.0 349.1 jit_solution(17713936069963146569)
XLA Ops:
  7.2 5.4 %fusion.65 = (bf16[16,2048]{1,0:T(8,128)(2,1)}, f32[16,2048]{1,0:T(8,128)S(1)}) fusion(bf16[2048,2048]{1,0:T(8,128)(2,1)} %param.24, bf16[2,16,2048]{2,1,0:T(8,128)(2,1)} %param.23, f32[16,2048]{1,0:T(8,128)} %param.22, f32[2048]{0:T(1024)} %param.25), kind=kOutput, calls=%fused_computation.112 | convolution fusion | flops 134316032 | bytes 8790016 | tf_op jit(solution)/shard_map/dot_general | solution.py:61
  13.1 1.9 fusion.64
  15.1 0.7 all-gather.3.cloned.1.call-update
  16.2 4.5 %copy.13 = bf16[128,64,64]{1,2,0:T(8,128)(2,1)} copy(bf16[128,64,64]{0,2,1:T(8,128)(2,1)S(1)} %copy-done.1) | data formatting | bytes 2097152 | tf_op args[6]
  20.7 45.6 %all-gather.5.cloned.1.call-done = bf16[512,2048]{1,0:T(8,128)(2,1)} async-done(((bf16[16,2048]{1,0:T(8,128)(2,1)}), bf16[512,2048]{1,0:T(8,128)(2,1)}) %all-gather.5.cloned.1.call-update) | async-done | bytes 2097168 | tf_op jit(solution)/shard_map/all_gather | solution.py:66
  66.3 2.9 copy.17
  69.2 52.6 %while.21 = (s32[]{:T(128)}, f32[8,16,512]{2,1,0:T(8,128)S(1)}, s32[8,16,64]{2,1,0:T(8,128)S(1)}, bf16[512,2048]{0,1:T(8,128)(2,1)S(1)}, bf16[8,16,64]{2,1,0:T(8...) while((s32[]{:T(128)}, f32[8,16,512]{2,1,0:T(8,128)S(1)}, ...), condition=%wide.region_10.16_spmd, body=%wide.region_8.15_spmd.sunk | while | flops 70291552 | bytes 6755201 | solution.py:29
  69.4 0.6 gather_fusion.3
  70.0 4.0 %gather_fusion.2 = bf16[1024,512]{1,0:T(8,128)(2,1)S(1)} fusion(bf16[512,2048]{0,1:T(8,128)(2,1)S(1)} %get-tuple-element.254, s32[1024]{0:T(1024)S(1)} %fusion.90), kind=kCustom, calls=%fused_computation.2.clone.clone.1 | custom fusion | bytes 2101248 | tf_op jit(solution)/shard_map/while/body/eval_jaxpr/jit(_take)/gather | solution.py:16
  74.2 1.5 fusion.91
  76.0 0.6 gather_fusion.3
  76.6 4.0 %gather_fusion.2 = bf16[1024,512]{1,0:T(8,128)(2,1)S(1)} fusion(bf16[512,2048]{0,1:T(8,128)(2,1)S(1)} %get-tuple-element.254, s32[1024]{0:T(1024)S(1)} %fusion.90), kind=kCustom, calls=%fused_computation.2.clone.clone.1 | custom fusion | bytes 2101248 | tf_op jit(solution)/shard_map/while/body/eval_jaxpr/jit(_take)/gather | solution.py:16
  80.7 1.5 fusion.91
  82.5 0.6 gather_fusion.3
  83.1 4.0 %gather_fusion.2 = bf16[1024,512]{1,0:T(8,128)(2,1)S(1)} fusion(bf16[512,2048]{0,1:T(8,128)(2,1)S(1)} %get-tuple-element.254, s32[1024]{0:T(1024)S(1)} %fusion.90), kind=kCustom, calls=%fused_computation.2.clone.clone.1 | custom fusion | bytes 2101248 | tf_op jit(solution)/shard_map/while/body/eval_jaxpr/jit(_take)/gather | solution.py:16
  87.3 1.5 fusion.91
  89.7 4.0 %gather_fusion.2 = bf16[1024,512]{1,0:T(8,128)(2,1)S(1)} fusion(bf16[512,2048]{0,1:T(8,128)(2,1)S(1)} %get-tuple-element.254, s32[1024]{0:T(1024)S(1)} %fusion.90), kind=kCustom, calls=%fused_computation.2.clone.clone.1 | custom fusion | bytes 2101248 | tf_op jit(solution)/shard_map/while/body/eval_jaxpr/jit(_take)/gather | solution.py:16
  93.9 1.5 fusion.91
  96.3 4.0 %gather_fusion.2 = bf16[1024,512]{1,0:T(8,128)(2,1)S(1)} fusion(bf16[512,2048]{0,1:T(8,128)(2,1)S(1)} %get-tuple-element.254, s32[1024]{0:T(1024)S(1)} %fusion.90), kind=kCustom, calls=%fused_computation.2.clone.clone.1 | custom fusion | bytes 2101248 | tf_op jit(solution)/shard_map/while/body/eval_jaxpr/jit(_take)/gather | solution.py:16
  100.5 1.5 fusion.91
  102.8 4.0 %gather_fusion.2 = bf16[1024,512]{1,0:T(8,128)(2,1)S(1)} fusion(bf16[512,2048]{0,1:T(8,128)(2,1)S(1)} %get-tuple-element.254, s32[1024]{0:T(1024)S(1)} %fusion.90), kind=kCustom, calls=%fused_computation.2.clone.clone.1 | custom fusion | bytes 2101248 | tf_op jit(solution)/shard_map/while/body/eval_jaxpr/jit(_take)/gather | solution.py:16
  107.0 1.5 fusion.91
  109.4 4.0 %gather_fusion.2 = bf16[1024,512]{1,0:T(8,128)(2,1)S(1)} fusion(bf16[512,2048]{0,1:T(8,128)(2,1)S(1)} %get-tuple-element.254, s32[1024]{0:T(1024)S(1)} %fusion.90), kind=kCustom, calls=%fused_computation.2.clone.clone.1 | custom fusion | bytes 2101248 | tf_op jit(solution)/shard_map/while/body/eval_jaxpr/jit(_take)/gather | solution.py:16
  113.6 1.5 fusion.91
  116.0 4.0 %gather_fusion.2 = bf16[1024,512]{1,0:T(8,128)(2,1)S(1)} fusion(bf16[512,2048]{0,1:T(8,128)(2,1)S(1)} %get-tuple-element.254, s32[1024]{0:T(1024)S(1)} %fusion.90), kind=kCustom, calls=%fused_computation.2.clone.clone.1 | custom fusion | bytes 2101248 | tf_op jit(solution)/shard_map/while/body/eval_jaxpr/jit(_take)/gather | solution.py:16
  120.2 1.5 fusion.91
  121.8 0.7 copy-done.2
  122.5 2.9 copy.14
  125.4 52.6 %while.20 = (s32[]{:T(128)}, f32[8,16,512]{2,1,0:T(8,128)S(1)}, s32[8,16,64]{2,1,0:T(8,128)S(1)}, bf16[512,2048]{0,1:T(8,128)(2,1)S(1)}, bf16[8,16,64]{2,1,0:T(8...) while((s32[]{:T(128)}, f32[8,16,512]{2,1,0:T(8,128)S(1)}, ...), condition=%wide.region_2.5_spmd, body=%wide.region_0.4_spmd.sunk | while | flops 70291552 | bytes 6755201 | solution.py:29
  126.2 4.0 %gather_fusion = bf16[1024,512]{1,0:T(8,128)(2,1)S(1)} fusion(bf16[512,2048]{0,1:T(8,128)(2,1)S(1)} %get-tuple-element.278, s32[1024]{0:T(1024)S(1)} %fusion.86), kind=kCustom, calls=%fused_computation.clone.clone.1 | custom fusion | bytes 2101248 | tf_op jit(solution)/shard_map/while/body/eval_jaxpr/jit(_take)/gather | solution.py:16
  130.4 1.5 fusion.87
  132.8 4.0 %gather_fusion = bf16[1024,512]{1,0:T(8,128)(2,1)S(1)} fusion(bf16[512,2048]{0,1:T(8,128)(2,1)S(1)} %get-tuple-element.278, s32[1024]{0:T(1024)S(1)} %fusion.86), kind=kCustom, calls=%fused_computation.clone.clone.1 | custom fusion | bytes 2101248 | tf_op jit(solution)/shard_map/while/body/eval_jaxpr/jit(_take)/gather | solution.py:16
  136.9 1.5 fusion.87
  139.3 4.0 %gather_fusion = bf16[1024,512]{1,0:T(8,128)(2,1)S(1)} fusion(bf16[512,2048]{0,1:T(8,128)(2,1)S(1)} %get-tuple-element.278, s32[1024]{0:T(1024)S(1)} %fusion.86), kind=kCustom, calls=%fused_computation.clone.clone.1 | custom fusion | bytes 2101248 | tf_op jit(solution)/shard_map/while/body/eval_jaxpr/jit(_take)/gather | solution.py:16
  143.5 1.5 fusion.87
  145.9 4.0 %gather_fusion = bf16[1024,512]{1,0:T(8,128)(2,1)S(1)} fusion(bf16[512,2048]{0,1:T(8,128)(2,1)S(1)} %get-tuple-element.278, s32[1024]{0:T(1024)S(1)} %fusion.86), kind=kCustom, calls=%fused_computation.clone.clone.1 | custom fusion | bytes 2101248 | tf_op jit(solution)/shard_map/while/body/eval_jaxpr/jit(_take)/gather | solution.py:16
  150.1 1.5 fusion.87
  152.5 4.0 %gather_fusion = bf16[1024,512]{1,0:T(8,128)(2,1)S(1)} fusion(bf16[512,2048]{0,1:T(8,128)(2,1)S(1)} %get-tuple-element.278, s32[1024]{0:T(1024)S(1)} %fusion.86), kind=kCustom, calls=%fused_computation.clone.clone.1 | custom fusion | bytes 2101248 | tf_op jit(solution)/shard_map/while/body/eval_jaxpr/jit(_take)/gather | solution.py:16
  156.7 1.5 fusion.87
  159.0 4.0 %gather_fusion = bf16[1024,512]{1,0:T(8,128)(2,1)S(1)} fusion(bf16[512,2048]{0,1:T(8,128)(2,1)S(1)} %get-tuple-element.278, s32[1024]{0:T(1024)S(1)} %fusion.86), kind=kCustom, calls=%fused_computation.clone.clone.1 | custom fusion | bytes 2101248 | tf_op jit(solution)/shard_map/while/body/eval_jaxpr/jit(_take)/gather | solution.py:16
  163.2 1.5 fusion.87
  165.6 4.0 %gather_fusion = bf16[1024,512]{1,0:T(8,128)(2,1)S(1)} fusion(bf16[512,2048]{0,1:T(8,128)(2,1)S(1)} %get-tuple-element.278, s32[1024]{0:T(1024)S(1)} %fusion.86), kind=kCustom, calls=%fused_computation.clone.clone.1 | custom fusion | bytes 2101248 | tf_op jit(solution)/shard_map/while/body/eval_jaxpr/jit(_take)/gather | solution.py:16
  169.8 1.5 fusion.87
  172.2 4.0 %gather_fusion = bf16[1024,512]{1,0:T(8,128)(2,1)S(1)} fusion(bf16[512,2048]{0,1:T(8,128)(2,1)S(1)} %get-tuple-element.278, s32[1024]{0:T(1024)S(1)} %fusion.86), kind=kCustom, calls=%fused_computation.clone.clone.1 | custom fusion | bytes 2101248 | tf_op jit(solution)/shard_map/while/body/eval_jaxpr/jit(_take)/gather | solution.py:16
  176.4 1.5 fusion.87
  178.0 1.2 fusion.19
  179.2 2.2 fusion.18
  181.4 0.9 slice_bitcast_fusion.1
  182.6 0.9 slice_bitcast_fusion
  183.9 113.8 %all-reduce.6.cloned.1.call-done = (f32[256,512]{1,0:T(8,128)}, f32[256,512]{1,0:T(8,128)}) async-done(((f32[256,512]{1,0:T(8,128)}, f32[256,512]{1,0:T(8,128)}), (f32[256,512]{1,0:T(8,128)}, f32[256,512]{1,0:T(8,128)})) %all-reduce.6.cloned.1.call-update) | async-done | bytes 1048592 | tf_op jit(solution)/shard_map/psum | solution.py:75
  297.7 1.1 fusion.20
  298.7 1.1 fusion.25
  299.8 30.7 %all-reduce.3 = (f32[17,17]{0,1:T(8,128)S(1)}, f32[17,8]{1,0:T(8,128)S(1)}, f32[17,17]{0,1:T(8,128)S(1)}, f32[17,8]{1,0:T(8,128)S(1)}) all-reduce(f32[17,17]{0,1:T(8,128)S(1)} %fusion.22, f32[17,8]{1,0:T(8,128)S(1)} %fusion.20, f32[17,17]{0,1:T(8,128)S(1)} %fusion.27, ...), channel_id=1, replica_groups=mesh['set'=32,'path'=8] {'path'}, use_global_device_ids=true, to_apply=%region_12.18 | all-reduce | flops 850 | bytes 6800 | tf_op jit(solution)/shard_map/psum | solution.py:79
  330.6 1.5 cholesky.55
  332.2 0.6 compare_reduce_fusion
  332.9 0.6 fusion.39
  333.5 1.3 custom-call.13
  335.2 1.1 fusion.14
  336.4 1.5 cholesky.44
  337.9 0.6 compare_reduce_fusion.1
  338.6 0.6 fusion.38
  339.2 1.3 custom-call.11
  340.9 1.1 fusion.17
  342.0 0.6 pad_maximum_fusion
  (198 shorter events, 17.0 us)
Async XLA Ops:
  7.2 5.4 %copy-start.4 = (f32[2048]{0:T(1024)S(1)}, f32[2048]{0:T(1024)}, u32[]{:S(2)}) copy-start(f32[2048]{0:T(1024)} %param.25) | copy-start | bytes 24580
  7.2 5.4 %copy-start.3 = (bf16[2,16,2048]{2,1,0:T(8,128)(2,1)S(1)}, bf16[2,16,2048]{2,1,0:T(8,128)(2,1)}, u32[]{:S(2)}) copy-start(bf16[2,16,2048]{2,1,0:T(8,128)(2,1)} %param.23) | copy-start | bytes 393220
  7.2 59.2 %all-gather.5.cloned.1.call-start = ((), (), s32[]{:S(2)}) async-start(), calls=%async_computation.1 | async-start | bytes 2162688 | tf_op jit(solution)/shard_map/all_gather | solution.py:66
  7.2 5.9 %copy-start = (bf16[2048,2048]{1,0:T(8,128)(2,1)S(1)}, bf16[2048,2048]{1,0:T(8,128)(2,1)}, u32[]{:S(2)}) copy-start(bf16[2048,2048]{1,0:T(8,128)(2,1)} %param.24) | copy-start | bytes 25165828
  13.1 2.7 copy-start.8
  13.1 2.8 copy-start.6
  13.1 2.9 copy-start.5
  13.1 3.0 copy-start.1
  15.0 106.8 %all-gather.3.cloned.1.call-start = ((), (), s32[]{:S(2)}) async-start(), calls=%async_computation | async-start | bytes 2162688 | tf_op jit(solution)/shard_map/all_gather | solution.py:66
  15.8 281.9 %all-reduce.6.cloned.1.call-start = ((), (), s32[]{:S(2)}) async-start(), calls=%async_computation.2 | async-start | bytes 2097152 | tf_op jit(solution)/shard_map/psum | solution.py:75
  121.8 0.7 copy-start.2
  125.4 52.6 %copy-start.7 = (s32[128]{0:T(128)S(1)}, s32[128]{0:T(128)}, u32[]{:S(2)}) copy-start(s32[128]{0:T(128)} %param.30) | copy-start | bytes 1540
Sparse Core Ops, SparseCore 0:
  15.2 51.1 all-gather.4
  68.9 47.9 all-gather.2
  181.5 116.0 all-reduce.5
where the time goes:
time: 350 us; the launch traced here: 349 us
  waiting for transfers between devices  160 us (46%)
  local copies, waits for them, and re-layouts  87.9 us (25%)
  matrix products  40.6 us (12%)
  blocking collectives  30.7 us (9%)
  other arithmetic  14.4 us (4%)
  between operations  14 us (4%)
    psum x1, waiting for transfers between devices, per_device(): summed = lax.psum(jnp.dot(onehot, values, precision=high), 'set')  114 us
    gather x16, local copies, waits for them, and re-layouts, value_block(): jnp.take(slab, lists_b.reshape(-1), axis=1)  63.4 us
    all_gather x2, waiting for transfers between devices, per_device(): piece = lax.all_gather(slab, 'set', axis=0, tiled=True)  45.7 us
    psum x1, blocking collectives, per_device(): lax.psum((jnp.dot(basis, basis.T, precision=high), jnp.dot(basis, netted....  30.7 us
    dot_general x16, matrix products, value_block(): jnp.einsum('psk,skl->psl', picked, gamma_b, preferred_element_type=jnp.fl...  24.4 us
    gather x16, local copies, waits for them, and re-layouts, value_block(): rates = jnp.exp(0.2 * jnp.take(slab, cur_b, axis=1).astype(jnp.float32))  9.44 us
    dot_general x2, matrix products, per_device(): jnp.dot(shocks[step], loading, preferred_element_type=jnp.float32)  7.25 us
  transfers between devices with their start and end apart: 3, of which 2 were waited for; matrix products, arithmetic and copies ran while one was open for 18% of the time, Pallas kernels for 0%

commit v1 on v0

--- a/solution.py
+++ b/solution.py
@@ -72,7 +72,9 @@
     for step in range(STEPS):
         values = evaluated[step][:set_count]
         factors = evaluated[step][set_count:]
-        summed = lax.psum(jnp.dot(onehot, values, precision=high), "set")
+        part = jnp.dot(onehot, values, precision=high)
+        terms = lax.all_gather(part, "set", axis=0, tiled=False)
+        summed = terms.sum(axis=0)
         netted = lax.dynamic_slice_in_dim(summed, member * CP_DEV, CP_DEV, 0)
         ones = jnp.ones((1, values.shape[1]), jnp.float32)
         basis = jnp.concatenate([ones, factors], axis=0)

time: 350 us -> 334 us (0.954)
  waiting for transfers between devices: 160 us -> 130 us
  other arithmetic: 14.4 us -> 29.9 us
    psum x1 -> x0, waiting for transfers between devices: 114 us -> none  [per_device(): summed = lax.psum(jnp.dot(onehot, values, precision=high), 'set')]
    all_gather x0 -> x2, waiting for transfers between devices: none -> 89.4 us  [per_device(): terms = lax.all_gather(part, 'set', axis=0, tiled=False)]
    reduce_sum x0 -> x2, other arithmetic: none -> 15.5 us  [per_device(): summed = terms.sum(axis=0)]
    all_gather x2, waiting for transfers between devices: 45.7 us -> 40.9 us  [per_device(): piece = lax.all_gather(slab, 'set', axis=0, tiled=True)]
  transfers between devices with their start and end apart: 3 -> 4, of which waited for: 2 -> 3; matrix products, arithmetic and copies ran while one was open for 18% -> 40% of each run, Pallas kernels for 0% -> 0%
where the time goes in v1:
time: 334 us
  waiting for transfers between devices  130 us (39%)
  local copies, waits for them, and re-layouts  86.8 us (26%)
  matrix products  40.1 us (12%)
  blocking collectives  30.7 us (9%)
  other arithmetic  29.9 us (9%)
  between operations  14 us (4%)
    all_gather x2, waiting for transfers between devices, per_device(): terms = lax.all_gather(part, 'set', axis=0, tiled=False)  89.4 us
    gather x16, local copies, waits for them, and re-layouts, value_block(): jnp.take(slab, lists_b.reshape(-1), axis=1)  63.4 us
    all_gather x2, waiting for transfers between devices, per_device(): piece = lax.all_gather(slab, 'set', axis=0, tiled=True)  40.9 us
    psum x1, blocking collectives, per_device(): lax.psum((jnp.dot(basis, basis.T, precision=high), jnp.dot(basis, netted....  30.7 us
    dot_general x16, matrix products, value_block(): jnp.einsum('psk,skl->psl', picked, gamma_b, preferred_element_type=jnp.fl...  24.4 us
    reduce_sum x2, other arithmetic, per_device(): summed = terms.sum(axis=0)  15.5 us
    dot_general x2, matrix products, per_device(): jnp.dot(shocks[step], loading, preferred_element_type=jnp.float32)  10.6 us
    gather x16, local copies, waits for them, and re-layouts, value_block(): rates = jnp.exp(0.2 * jnp.take(slab, cur_b, axis=1).astype(jnp.float32))  9.44 us
  transfers between devices with their start and end apart: 4, of which 3 were waited for; matrix products, arithmetic and copies ran while one was open for 40% of the time, Pallas kernels for 0%

profile of v1, /device:TPU:6, one launch (start us, length us, event | category | flops | bytes accessed | tf_op | source)
XLA Modules:
  0.0 333.5 jit_solution(13971584882055103625)
XLA Ops:
  7.2 5.2 %fusion.65 = (bf16[16,2048]{1,0:T(8,128)(2,1)}, f32[16,2048]{1,0:T(8,128)S(1)}) fusion(bf16[2048,2048]{1,0:T(8,128)(2,1)} %param.24, bf16[2,16,2048]{2,1,0:T(8,128)(2,1)} %param.23, f32[16,2048]{1,0:T(8,128)} %param.22, f32[2048]{0:T(1024)} %param.25), kind=kOutput, calls=%fused_computation.112 | convolution fusion | flops 134316032 | bytes 8790016 | tf_op jit(solution)/shard_map/dot_general | solution.py:61
  12.6 5.3 %fusion.64 = (bf16[16,2048]{1,0:T(8,128)(2,1)}, f32[16,2048]{1,0:T(8,128)}) fusion(bf16[2048,2048]{1,0:T(8,128)(2,1)} %param.24, bf16[2,16,2048]{2,1,0:T(8,128)(2,1)S(1)} %copy-done.1, f32[16,2048]{1,0:T(8,128)S(1)} %get-tuple-element.136, f32[2048]{0:T(1024)S(1)} %copy-done.2), kind=kOutput, calls=%fused_computation.111 | convolution fusion | flops 134316032 | bytes 8790016 | tf_op jit(solution)/shard_map/dot_general | solution.py:61
  18.4 4.5 %copy.13 = bf16[128,64,64]{1,2,0:T(8,128)(2,1)} copy(bf16[128,64,64]{0,2,1:T(8,128)(2,1)S(1)} %copy-done) | data formatting | bytes 2097152 | tf_op args[6]
  22.9 40.9 %all-gather.7.cloned.1.call-done = bf16[512,2048]{1,0:T(8,128)(2,1)} async-done(((bf16[16,2048]{1,0:T(8,128)(2,1)}), bf16[512,2048]{1,0:T(8,128)(2,1)}) %all-gather.7.cloned.1.call-update) | async-done | bytes 2097168 | tf_op jit(solution)/shard_map/all_gather | solution.py:66
  63.8 2.9 copy.14
  66.7 52.6 %while.20 = (s32[]{:T(128)}, f32[8,16,512]{2,1,0:T(8,128)S(1)}, s32[8,16,64]{2,1,0:T(8,128)S(1)}, bf16[512,2048]{0,1:T(8,128)(2,1)S(1)}, bf16[8,16,64]{2,1,0:T(8...) while((s32[]{:T(128)}, f32[8,16,512]{2,1,0:T(8,128)S(1)}, ...), condition=%wide.region_2.5_spmd, body=%wide.region_0.4_spmd.sunk | while | flops 70291552 | bytes 6755201 | solution.py:29
  66.9 0.6 gather_fusion.1
  67.5 4.0 %gather_fusion = bf16[1024,512]{1,0:T(8,128)(2,1)S(1)} fusion(bf16[512,2048]{0,1:T(8,128)(2,1)S(1)} %get-tuple-element.276, s32[1024]{0:T(1024)S(1)} %fusion.86), kind=kCustom, calls=%fused_computation.clone.clone.1 | custom fusion | bytes 2101248 | tf_op jit(solution)/shard_map/while/body/eval_jaxpr/jit(_take)/gather | solution.py:16
  71.6 1.5 fusion.87
  73.4 0.6 gather_fusion.1
  74.0 4.0 %gather_fusion = bf16[1024,512]{1,0:T(8,128)(2,1)S(1)} fusion(bf16[512,2048]{0,1:T(8,128)(2,1)S(1)} %get-tuple-element.276, s32[1024]{0:T(1024)S(1)} %fusion.86), kind=kCustom, calls=%fused_computation.clone.clone.1 | custom fusion | bytes 2101248 | tf_op jit(solution)/shard_map/while/body/eval_jaxpr/jit(_take)/gather | solution.py:16
  78.2 1.5 fusion.87
  80.0 0.6 gather_fusion.1
  80.6 4.0 %gather_fusion = bf16[1024,512]{1,0:T(8,128)(2,1)S(1)} fusion(bf16[512,2048]{0,1:T(8,128)(2,1)S(1)} %get-tuple-element.276, s32[1024]{0:T(1024)S(1)} %fusion.86), kind=kCustom, calls=%fused_computation.clone.clone.1 | custom fusion | bytes 2101248 | tf_op jit(solution)/shard_map/while/body/eval_jaxpr/jit(_take)/gather | solution.py:16
  84.8 1.5 fusion.87
  86.6 0.6 gather_fusion.1
  87.2 4.0 %gather_fusion = bf16[1024,512]{1,0:T(8,128)(2,1)S(1)} fusion(bf16[512,2048]{0,1:T(8,128)(2,1)S(1)} %get-tuple-element.276, s32[1024]{0:T(1024)S(1)} %fusion.86), kind=kCustom, calls=%fused_computation.clone.clone.1 | custom fusion | bytes 2101248 | tf_op jit(solution)/shard_map/while/body/eval_jaxpr/jit(_take)/gather | solution.py:16
  91.4 1.5 fusion.87
  93.2 0.6 gather_fusion.1
  93.7 4.0 %gather_fusion = bf16[1024,512]{1,0:T(8,128)(2,1)S(1)} fusion(bf16[512,2048]{0,1:T(8,128)(2,1)S(1)} %get-tuple-element.276, s32[1024]{0:T(1024)S(1)} %fusion.86), kind=kCustom, calls=%fused_computation.clone.clone.1 | custom fusion | bytes 2101248 | tf_op jit(solution)/shard_map/while/body/eval_jaxpr/jit(_take)/gather | solution.py:16
  97.9 1.5 fusion.87
  99.7 0.6 gather_fusion.1
  100.3 4.0 %gather_fusion = bf16[1024,512]{1,0:T(8,128)(2,1)S(1)} fusion(bf16[512,2048]{0,1:T(8,128)(2,1)S(1)} %get-tuple-element.276, s32[1024]{0:T(1024)S(1)} %fusion.86), kind=kCustom, calls=%fused_computation.clone.clone.1 | custom fusion | bytes 2101248 | tf_op jit(solution)/shard_map/while/body/eval_jaxpr/jit(_take)/gather | solution.py:16
  104.5 1.5 fusion.87
  106.9 4.0 %gather_fusion = bf16[1024,512]{1,0:T(8,128)(2,1)S(1)} fusion(bf16[512,2048]{0,1:T(8,128)(2,1)S(1)} %get-tuple-element.276, s32[1024]{0:T(1024)S(1)} %fusion.86), kind=kCustom, calls=%fused_computation.clone.clone.1 | custom fusion | bytes 2101248 | tf_op jit(solution)/shard_map/while/body/eval_jaxpr/jit(_take)/gather | solution.py:16
  111.1 1.5 fusion.87
  113.5 4.0 %gather_fusion = bf16[1024,512]{1,0:T(8,128)(2,1)S(1)} fusion(bf16[512,2048]{0,1:T(8,128)(2,1)S(1)} %get-tuple-element.276, s32[1024]{0:T(1024)S(1)} %fusion.86), kind=kCustom, calls=%fused_computation.clone.clone.1 | custom fusion | bytes 2101248 | tf_op jit(solution)/shard_map/while/body/eval_jaxpr/jit(_take)/gather | solution.py:16
  117.7 1.5 fusion.87
  119.3 1.2 fusion.19
  120.8 2.9 copy.17
  123.7 52.6 %while.21 = (s32[]{:T(128)}, f32[8,16,512]{2,1,0:T(8,128)S(1)}, s32[8,16,64]{2,1,0:T(8,128)S(1)}, bf16[512,2048]{0,1:T(8,128)(2,1)S(1)}, bf16[8,16,64]{2,1,0:T(8...) while((s32[]{:T(128)}, f32[8,16,512]{2,1,0:T(8,128)S(1)}, ...), condition=%wide.region_10.16_spmd, body=%wide.region_8.15_spmd.sunk | while | flops 70291552 | bytes 6755201 | solution.py:29
  124.5 4.0 %gather_fusion.2 = bf16[1024,512]{1,0:T(8,128)(2,1)S(1)} fusion(bf16[512,2048]{0,1:T(8,128)(2,1)S(1)} %get-tuple-element.252, s32[1024]{0:T(1024)S(1)} %fusion.90), kind=kCustom, calls=%fused_computation.2.clone.clone.1 | custom fusion | bytes 2101248 | tf_op jit(solution)/shard_map/while/body/eval_jaxpr/jit(_take)/gather | solution.py:16
  128.6 1.5 fusion.91
  131.0 4.0 %gather_fusion.2 = bf16[1024,512]{1,0:T(8,128)(2,1)S(1)} fusion(bf16[512,2048]{0,1:T(8,128)(2,1)S(1)} %get-tuple-element.252, s32[1024]{0:T(1024)S(1)} %fusion.90), kind=kCustom, calls=%fused_computation.2.clone.clone.1 | custom fusion | bytes 2101248 | tf_op jit(solution)/shard_map/while/body/eval_jaxpr/jit(_take)/gather | solution.py:16
  135.2 1.5 fusion.91
  137.6 4.0 %gather_fusion.2 = bf16[1024,512]{1,0:T(8,128)(2,1)S(1)} fusion(bf16[512,2048]{0,1:T(8,128)(2,1)S(1)} %get-tuple-element.252, s32[1024]{0:T(1024)S(1)} %fusion.90), kind=kCustom, calls=%fused_computation.2.clone.clone.1 | custom fusion | bytes 2101248 | tf_op jit(solution)/shard_map/while/body/eval_jaxpr/jit(_take)/gather | solution.py:16
  141.8 1.5 fusion.91
  144.2 4.0 %gather_fusion.2 = bf16[1024,512]{1,0:T(8,128)(2,1)S(1)} fusion(bf16[512,2048]{0,1:T(8,128)(2,1)S(1)} %get-tuple-element.252, s32[1024]{0:T(1024)S(1)} %fusion.90), kind=kCustom, calls=%fused_computation.2.clone.clone.1 | custom fusion | bytes 2101248 | tf_op jit(solution)/shard_map/while/body/eval_jaxpr/jit(_take)/gather | solution.py:16
  148.4 1.5 fusion.91
  150.8 4.0 %gather_fusion.2 = bf16[1024,512]{1,0:T(8,128)(2,1)S(1)} fusion(bf16[512,2048]{0,1:T(8,128)(2,1)S(1)} %get-tuple-element.252, s32[1024]{0:T(1024)S(1)} %fusion.90), kind=kCustom, calls=%fused_computation.2.clone.clone.1 | custom fusion | bytes 2101248 | tf_op jit(solution)/shard_map/while/body/eval_jaxpr/jit(_take)/gather | solution.py:16
  154.9 1.5 fusion.91
  157.3 4.0 %gather_fusion.2 = bf16[1024,512]{1,0:T(8,128)(2,1)S(1)} fusion(bf16[512,2048]{0,1:T(8,128)(2,1)S(1)} %get-tuple-element.252, s32[1024]{0:T(1024)S(1)} %fusion.90), kind=kCustom, calls=%fused_computation.2.clone.clone.1 | custom fusion | bytes 2101248 | tf_op jit(solution)/shard_map/while/body/eval_jaxpr/jit(_take)/gather | solution.py:16
  161.5 1.5 fusion.91
  163.9 4.0 %gather_fusion.2 = bf16[1024,512]{1,0:T(8,128)(2,1)S(1)} fusion(bf16[512,2048]{0,1:T(8,128)(2,1)S(1)} %get-tuple-element.252, s32[1024]{0:T(1024)S(1)} %fusion.90), kind=kCustom, calls=%fused_computation.2.clone.clone.1 | custom fusion | bytes 2101248 | tf_op jit(solution)/shard_map/while/body/eval_jaxpr/jit(_take)/gather | solution.py:16
  168.1 1.5 fusion.91
  170.5 4.0 %gather_fusion.2 = bf16[1024,512]{1,0:T(8,128)(2,1)S(1)} fusion(bf16[512,2048]{0,1:T(8,128)(2,1)S(1)} %get-tuple-element.252, s32[1024]{0:T(1024)S(1)} %fusion.90), kind=kCustom, calls=%fused_computation.2.clone.clone.1 | custom fusion | bytes 2101248 | tf_op jit(solution)/shard_map/while/body/eval_jaxpr/jit(_take)/gather | solution.py:16
  174.7 1.5 fusion.91
  176.3 1.2 fusion.18
  177.5 0.9 slice_bitcast_fusion.1
  178.8 0.9 slice_bitcast_fusion
  180.0 18.0 %all-gather.11.cloned.1.call-done = f32[8192,512]{1,0:T(8,128)} async-done(((f32[256,512]{1,0:T(8,128)}), f32[8192,512]{1,0:T(8,128)}) %all-gather.11.cloned.1.call-update) | async-done | bytes 16777232 | tf_op jit(solution)/shard_map/all_gather | solution.py:76
  198.0 7.8 %reduce_sum.36 = f32[256,512]{1,0:T(8,128)S(1)} reduce(f32[32,256,512]{2,1,0:T(8,128)} %bitcast.139, f32[]{:T(128)} %constant.111.clone.1), dimensions={0}, to_apply=%region_3.6 | reduce | flops 4063232 | bytes 17301508 | tf_op jit(solution)/shard_map/reduce_sum | solution.py:77
  206.1 71.5 %all-gather.13.cloned.1.call-done = f32[8192,512]{1,0:T(8,128)} async-done(((f32[256,512]{1,0:T(8,128)}), f32[8192,512]{1,0:T(8,128)}) %all-gather.13.cloned.1.call-update) | async-done | bytes 16777232 | tf_op jit(solution)/shard_map/all_gather | solution.py:76
  277.5 7.8 %reduce_sum.37 = f32[256,512]{1,0:T(8,128)S(1)} reduce(f32[32,256,512]{2,1,0:T(8,128)} %bitcast.140, f32[]{:T(128)} %constant.111.clone.1), dimensions={0}, to_apply=%region_11.17 | reduce | flops 4063232 | bytes 17301508 | tf_op jit(solution)/shard_map/reduce_sum | solution.py:77
  285.6 30.7 %all-reduce.2 = (f32[17,17]{0,1:T(8,128)S(1)}, f32[17,8]{1,0:T(8,128)S(1)}, f32[17,17]{0,1:T(8,128)S(1)}, f32[17,8]{1,0:T(8,128)S(1)}) all-reduce(f32[17,17]{0,1:T(8,128)S(1)} %fusion.22, f32[17,8]{1,0:T(8,128)S(1)} %fusion.20, f32[17,17]{0,1:T(8,128)S(1)} %fusion.27, ...), channel_id=1, replica_groups=mesh['set'=32,'path'=8] {'path'}, use_global_device_ids=true, to_apply=%region_12.18 | all-reduce | flops 850 | bytes 6800 | tf_op jit(solution)/shard_map/psum | solution.py:81
  316.5 1.5 cholesky.55
  318.1 0.6 compare_reduce_fusion
  318.7 0.6 fusion.39
  319.4 1.3 custom-call.13
  321.5 1.5 cholesky.44
  323.1 0.6 compare_reduce_fusion.1
  323.7 0.6 fusion.38
  324.4 1.3 custom-call.11
  326.4 0.6 pad_maximum_fusion
  (199 shorter events, 16.4 us)
Async XLA Ops:
  7.2 5.4 %copy-start.2 = (f32[2048]{0:T(1024)S(1)}, f32[2048]{0:T(1024)}, u32[]{:S(2)}) copy-start(f32[2048]{0:T(1024)} %param.25) | copy-start | bytes 24580
  7.2 5.4 %copy-start.1 = (bf16[2,16,2048]{2,1,0:T(8,128)(2,1)S(1)}, bf16[2,16,2048]{2,1,0:T(8,128)(2,1)}, u32[]{:S(2)}) copy-start(bf16[2,16,2048]{2,1,0:T(8,128)(2,1)} %param.23) | copy-start | bytes 393220
  7.2 56.6 %all-gather.7.cloned.1.call-start = ((), (), s32[]{:S(2)}) async-start(), calls=%async_computation | async-start | bytes 2162688 | tf_op jit(solution)/shard_map/all_gather | solution.py:66
  12.5 108.3 %all-gather.9.cloned.1.call-start = ((), (), s32[]{:S(2)}) async-start(), calls=%async_computation.1 | async-start | bytes 2162688 | tf_op jit(solution)/shard_map/all_gather | solution.py:66
  12.6 5.5 %copy-start.6 = (s32[128]{0:T(128)S(1)}, s32[128]{0:T(128)}, u32[]{:S(2)}) copy-start(s32[128]{0:T(128)} %param.29) | copy-start | bytes 1540
  12.6 5.5 %copy-start.4 = (bf16[128,64]{0,1:T(8,128)(2,1)S(1)}, bf16[128,64]{0,1:T(8,128)(2,1)}, u32[]{:S(2)}) copy-start(bf16[128,64]{0,1:T(8,128)(2,1)} %param.27) | copy-start | bytes 49156
  12.6 5.7 %copy-start.3 = (s32[128,64]{0,1:T(8,128)S(1)}, s32[128,64]{0,1:T(8,128)}, u32[]{:S(2)}) copy-start(s32[128,64]{0,1:T(8,128)} %param.26) | copy-start | bytes 98308
  12.6 5.7 %copy-start = (bf16[128,64,64]{0,2,1:T(8,128)(2,1)S(1)}, bf16[128,64,64]{0,2,1:T(8,128)(2,1)}, u32[]{:S(2)}) copy-start(bf16[128,64,64]{0,2,1:T(8,128)(2,1)} %param.28) | copy-start | bytes 3145732
  18.0 180.0 %all-gather.11.cloned.1.call-start = ((), (), s32[]{:S(2)}) async-start(), calls=%async_computation.2 | async-start | bytes 17301504 | tf_op jit(solution)/shard_map/all_gather | solution.py:76
  66.7 52.6 %copy-start.5 = (s32[128]{0:T(128)S(1)}, s32[128]{0:T(128)}, u32[]{:S(2)}) copy-start(s32[128]{0:T(128)} %param.30) | copy-start | bytes 1540
  120.5 157.0 %all-gather.13.cloned.1.call-start = ((), (), s32[]{:S(2)}) async-start(), calls=%async_computation.3 | async-start | bytes 17301504 | tf_op jit(solution)/shard_map/all_gather | solution.py:76
Sparse Core Ops, SparseCore 0:
  12.6 51.1 all-gather.6
  66.3 47.9 all-gather.8
  120.7 77.2 all-gather.10
  200.4 77.0 all-gather.12
